TPU v7x, 32 devices: a whole 2x2x4 slice. The times are simulated.
32 devices in a mesh: section: 4 (over y, x), dp: 2 (over core), tensor: 4 (over z).
Axes of the slice: x: 2, y: 2, z: 4, core: 2. Of those that a mesh axis runs over, the one named last changes fastest.
Arguments:
- cotangent: bfloat16 [2, 256, 8192], P(None, 'dp', 'tensor'), may hold values from -6 to 6
- stash: bfloat16 [4, 2, 256, 8192], P('section', None, 'dp', 'tensor'), may hold values from -0.25 to 0.25
- factor_a: bfloat16 [4, 1024, 8192], P('section', 'dp', 'tensor'), may hold values from -0.0625 to 0.0625
- factor_b: bfloat16 [4, 8192, 1024], P('section', ('tensor', 'dp')), may hold values from -0.1875 to 0.1875
- block_vals: bfloat16 [4, 8, 128, 128], P('section', ('dp', 'tensor')), may hold values from -0.25 to 0.25
- block_rows: int32 [4, 8], P('section'), may hold values from 0 to 63, as said below
- block_cols: int32 [4, 8], P('section'), may hold values from 0 to 63, as said below
Outputs:
- grad_in: bfloat16 [4, 2, 256, 8192], P('section', None, 'dp', 'tensor')
- block_grad: float32 [4, 8, 128, 128], P('section', ('dp', 'tensor'))
Inputs may be any that keep to these rules, and one draw needn't show every extreme that they name: The support lies inside the diagonal part of each tensor shard. Within a section all (block_rows, block_cols) pairs are distinct. For every dp index o < 2, tensor index t < 4 and slot k < 1, the block at position (o * 4 + t) + k has both its row and its column block index in [t * 8192 // (128 * 4), (t + 1) * 8192 // (128 * 4)). `block_cols`: drawn together with block_rows; the same promise holds.
All inputs are finite; a program needn't handle non-finite values.
Results may differ from a plain program's by a relative error of at most 0.024.
Values may be sent and summed in bfloat16 or wider, within the bound.
A program may use at most 128 MiB of HBM per device.

v0:
```python
import jax
import jax.numpy as jnp
from jax import lax
from jax.sharding import PartitionSpec as P


def shifted(value, axis, steps):
    count = lax.axis_size(axis)
    initial, last = (max(0, -steps), min(count, count - steps))
    return lax.ppermute(value, axis, [(source, source + steps) for source in range(initial, last)])


def pass_back(grad_out):
    return shifted(grad_out, "section", -1)


def on_device(cotangent, stash, factor_a, factor_b, block_vals, block_rows, block_cols):
    sections = lax.axis_size("section")
    section_pos = lax.axis_index("section")
    tensor_pos = lax.axis_index("tensor")
    dp_count = lax.axis_size("dp")
    tensor_count = lax.axis_size("tensor")
    left_full, right_full, values = (
        lax.all_gather(factor_a[0], "dp", axis=0, tiled=True),
        lax.all_gather(factor_b[0], "dp", axis=0, tiled=True),
        lax.all_gather(block_vals[0], "dp", axis=0, tiled=True),
    )
    batches = stash.shape[1]
    tokens_here = stash.shape[2]
    local_width = stash.shape[3]
    block_size = block_vals.shape[-1]
    local_blocks = local_width // block_size

    def local_ids(table):
        grid = table[0].reshape(dp_count, tensor_count, -1)
        mine = lax.dynamic_index_in_dim(grid, tensor_pos, 1, keepdims=False)
        return mine.reshape(-1) - tensor_pos * local_blocks

    positions = jnp.arange(local_blocks, dtype=jnp.int32)[None, :]
    row_hits = local_ids(block_rows)[:, None] == positions
    col_hits = local_ids(block_cols)[:, None] == positions
    row_pick = row_hits.astype(jnp.bfloat16)
    row_double = jnp.concatenate([row_pick, row_pick], axis=0)
    col_pick = col_hits.astype(jnp.bfloat16)
    grad_sum = jnp.zeros((values.shape[0], block_size, block_size), jnp.float32)
    grads_in = jnp.zeros(stash.shape[1:], jnp.bfloat16)
    received = jnp.zeros((tokens_here, local_width), jnp.bfloat16)
    steps = batches + sections - 1
    for step_idx in range(steps):
        batch_pos = step_idx - (sections - 1 - section_pos)
        active = (batch_pos >= 0) & (batch_pos < batches)
        slot_pos = jnp.clip(batch_pos, 0, batches - 1)
        fresh = lax.dynamic_index_in_dim(cotangent, slot_pos, 0, keepdims=False)
        cot_now = jnp.where(section_pos == sections - 1, fresh, received)
        partial_value = jnp.einsum(
            "td,rd->tr", cot_now, left_full, preferred_element_type=jnp.float32
        )
        share = lax.psum_scatter(
            partial_value.astype(jnp.bfloat16), "tensor", scatter_dimension=1, tiled=True
        )
        rank_act = lax.all_gather(share, "tensor", axis=1, tiled=True)
        picked_cot = jnp.einsum(
            "tlc,nl->tnc",
            cot_now.reshape(tokens_here, local_blocks, block_size),
            col_pick,
            preferred_element_type=jnp.float32,
        ).astype(jnp.bfloat16)
        sparse_terms = jnp.einsum(
            "tnc,nrc->tnr", picked_cot, values, preferred_element_type=jnp.float32
        )
        upper_part = sparse_terms.astype(jnp.bfloat16)
        lower_part = (sparse_terms - upper_part.astype(jnp.float32)).astype(jnp.bfloat16)
        both_parts = jnp.concatenate([upper_part, lower_part], axis=1)
        sparse_grad = jnp.einsum(
            "tnr,nl->tlr", both_parts, row_double, preferred_element_type=jnp.float32
        )
        dense_grad = jnp.einsum(
            "tr,dr->td", rank_act, right_full, preferred_element_type=jnp.float32
        )
        grad_out = (dense_grad + sparse_grad.reshape(tokens_here, local_width)).astype(jnp.bfloat16)
        current = lax.dynamic_index_in_dim(grads_in, slot_pos, 0, keepdims=False)
        grads_in = lax.dynamic_update_index_in_dim(
            grads_in, jnp.where(active, grad_out, current), slot_pos, 0
        )
        stash_now = lax.dynamic_index_in_dim(stash[0], slot_pos, 0, keepdims=False)
        live_scale = active.astype(jnp.bfloat16)
        if step_idx + 1 < steps:
            received = pass_back(grad_out)
        picked_in = (
            jnp.einsum(
                "tlr,nl->tnr",
                stash_now.reshape(tokens_here, local_blocks, block_size),
                row_pick,
                preferred_element_type=jnp.float32,
            ).astype(jnp.bfloat16)
            * live_scale
        )
        grad_sum = grad_sum + jnp.einsum(
            "tnr,tnc->nrc", picked_in, picked_cot, preferred_element_type=jnp.float32
        )
    block_grad = lax.psum_scatter(
        grad_sum.astype(jnp.bfloat16), "dp", scatter_dimension=0, tiled=True
    ).astype(jnp.float32)
    return (grads_in[None], block_grad[None])


def solution(mesh):
    in_specs = (
        P(None, "dp", "tensor"),
        P("section", None, "dp", "tensor"),
        P("section", "dp", "tensor"),
        P("section", ("tensor", "dp"), None),
        P("section", ("dp", "tensor"), None, None),
        P("section", None),
        P("section", None),
    )
    out_specs = (P("section", None, "dp", "tensor"), P("section", ("dp", "tensor"), None, None))
    return jax.shard_map(
        on_device, mesh=mesh, in_specs=in_specs, out_specs=out_specs, check_vma=False
    )
```

profile of v0, /device:TPU:0, one launch (start us, length us, event | category | flops | bytes accessed | tf_op | source)
XLA Modules:
  0.0 300.2 jit_solution(10202126768568250833)
XLA Ops:
  8.0 17.9 %all-gather.6.cloned.1.call-done = bf16[1,1024,2048]{2,1,0:T(8,128)(2,1)} async-done(((bf16[1,512,2048]{2,1,0:T(8,128)(2,1)}), bf16[1,1024,2048]{2,1,0:T(8,128)(2,1)}) %all-gather.6.cloned.1.call-update) | async-done | bytes 4194320 | tf_op jit(solution)/shard_map/all_gather | solution.py:24
  25.9 4.6 %fusion.59 = bf16[128,1024]{1,0:T(8,128)(2,1)} fusion(bf16[1,1024,2048]{2,1,0:T(8,128)(2,1)} %all-gather.6.cloned.1.call-done, bf16[2,128,2048]{2,1,0:T(8,128)(2,1)} %param.7, s32[]{:T(128)S(6)} %min.16, pred[]{:T(512)S(6)} %eq.14), kind=kOutput, calls=%fused_computation.33 | convolution fusion | flops 537264128 | bytes 4980741 | tf_op jit(solution)/shard_map/td,rd->tr/dot_general | solution.py:55
  33.6 1.5 dynamic-slice_bitcast_fusion
  36.2 1.9 all-gather.2
  39.0 12.9 %reduce-scatter.7.cloned.1.call-done = bf16[128,256]{1,0:T(8,128)(2,1)} async-done(((bf16[128,1024]{1,0:T(8,128)(2,1)}), bf16[128,256]{1,0:T(8,128)(2,1)}) %reduce-scatter.7.cloned.1.call-update) | async-done | bytes 65552 | tf_op jit(solution)/shard_map/reduce_scatter | solution.py:58
  51.9 14.0 %all_gather.25 = bf16[128,1024]{1,0:T(8,128)(2,1)S(1)} all-gather(bf16[128,256]{1,0:T(8,128)(2,1)} %reduce-scatter.7.cloned.1.call-done), channel_id=1, replica_groups=mesh['section'=4,'dp'=2,'tensor'=4] {'tensor'}, dimensions={1}, use_global_device_ids=true | all-gather | bytes 327680 | tf_op jit(solution)/shard_map/all_gather | solution.py:61
  66.0 4.7 %bitcast_dynamic-update-slice_fusion.3 = (bf16[2,128,2048]{2,1,0:T(8,128)(2,1)S(1)}, bf16[128,2048]{1,0:T(8,128)(2,1)}) fusion(bf16[2,128,2048]{2,1,0:T(8,128)(2,1)S(1)} %broadcast_in_dim.36, s32[]{:T(128)S(6)} %min.16, pred[]{:T(512)S(6)} %and.17, f32[16,8,16,128]{3,2,1,0:T(8,128)S(1)} %bitcast.277, bf16[128,1024]{1,0:T(8,128)(2,1)S(1)} %all_gather.25, ...), kind=kOutput, calls=%fused_computation.83 | convolution fusion | flops 537657344 | bytes 6553605 | tf_op jit(solution)/shard_map/tr,dr->td/dot_general | solution.py:77
  70.7 1.3 collective-permute-start
  72.0 2.0 fusion.81
  75.1 2.0 copy.73
  78.8 7.5 %collective-permute-done = bf16[128,2048]{1,0:T(8,128)(2,1)S(1)} collective-permute-done((bf16[128,2048]{1,0:T(8,128)(2,1)}, bf16[128,2048]{1,0:T(8,128)(2,1)S(1)}, u32[]{:S(2)}, u32[]{:S(2)}) %collective-permute-start) | collective-permute-done | bytes 524320 | tf_op jit(solution)/shard_map/ppermute | solution.py:10
  86.8 2.2 fusion.62
  89.8 20.7 %reduce-scatter.9.cloned.1.call-done = bf16[128,256]{1,0:T(8,128)(2,1)} async-done(((bf16[128,1024]{1,0:T(8,128)(2,1)}), bf16[128,256]{1,0:T(8,128)(2,1)}) %reduce-scatter.9.cloned.1.call-update) | async-done | bytes 65552 | tf_op jit(solution)/shard_map/reduce_scatter | solution.py:58
  110.4 14.2 %all_gather.28 = bf16[128,1024]{1,0:T(8,128)(2,1)S(1)} all-gather(bf16[128,256]{1,0:T(8,128)(2,1)} %reduce-scatter.9.cloned.1.call-done), channel_id=1, replica_groups=mesh['section'=4,'dp'=2,'tensor'=4] {'tensor'}, dimensions={1}, use_global_device_ids=true | all-gather | bytes 327680 | tf_op jit(solution)/shard_map/all_gather | solution.py:61
  124.6 4.8 %bitcast_dynamic-update-slice_fusion.2 = (bf16[2,128,2048]{2,1,0:T(8,128)(2,1)S(1)}, bf16[128,2048]{1,0:T(8,128)(2,1)}) fusion(bf16[2,128,2048]{2,1,0:T(8,128)(2,1)S(1)} %get-tuple-element.17, s32[]{:T(128)S(6)} %min.17, bf16[1,128,2048]{2,1,0:T(8,128)(2,1)} %constant_dynamic-slice_fusion.2, pred[]{:T(512)S(6)} %and.18, ...), kind=kOutput, calls=%fused_computation.80 | convolution fusion | flops 537657344 | bytes 7077893 | tf_op jit(solution)/shard_map/tr,dr->td/dot_general | solution.py:77
  134.6 6.4 %collective-permute-done.1 = bf16[128,2048]{1,0:T(8,128)(2,1)S(1)} collective-permute-done((bf16[128,2048]{1,0:T(8,128)(2,1)}, bf16[128,2048]{1,0:T(8,128)(2,1)S(1)}, u32[]{:S(2)}, u32[]{:S(2)}) %collective-permute-start.1) | collective-permute-done | bytes 524320 | tf_op jit(solution)/shard_map/ppermute | solution.py:10
  141.4 2.2 fusion.65
  144.4 17.8 %reduce-scatter.11.cloned.1.call-done = bf16[128,256]{1,0:T(8,128)(2,1)} async-done(((bf16[128,1024]{1,0:T(8,128)(2,1)}), bf16[128,256]{1,0:T(8,128)(2,1)}) %reduce-scatter.11.cloned.1.call-update) | async-done | bytes 65552 | tf_op jit(solution)/shard_map/reduce_scatter | solution.py:58
  162.2 14.4 %all_gather.29 = bf16[128,1024]{1,0:T(8,128)(2,1)S(1)} all-gather(bf16[128,256]{1,0:T(8,128)(2,1)} %reduce-scatter.11.cloned.1.call-done), channel_id=1, replica_groups=mesh['section'=4,'dp'=2,'tensor'=4] {'tensor'}, dimensions={1}, use_global_device_ids=true | all-gather | bytes 327680 | tf_op jit(solution)/shard_map/all_gather | solution.py:61
  176.6 4.8 %bitcast_dynamic-update-slice_fusion.1 = (bf16[2,128,2048]{2,1,0:T(8,128)(2,1)S(1)}, bf16[128,2048]{1,0:T(8,128)(2,1)}) fusion(bf16[2,128,2048]{2,1,0:T(8,128)(2,1)S(1)} %get-tuple-element.19, s32[]{:T(128)S(6)} %min.18, bf16[1,128,2048]{2,1,0:T(8,128)(2,1)} %constant_dynamic-slice_fusion.1, pred[]{:T(512)S(6)} %and.19, ...), kind=kOutput, calls=%fused_computation.77 | convolution fusion | flops 537657344 | bytes 7077893 | tf_op jit(solution)/shard_map/tr,dr->td/dot_general | solution.py:77
  186.6 6.2 %collective-permute-done.2 = bf16[128,2048]{1,0:T(8,128)(2,1)S(1)} collective-permute-done((bf16[128,2048]{1,0:T(8,128)(2,1)}, bf16[128,2048]{1,0:T(8,128)(2,1)S(1)}, u32[]{:S(2)}, u32[]{:S(2)}) %collective-permute-start.2) | collective-permute-done | bytes 524320 | tf_op jit(solution)/shard_map/ppermute | solution.py:10
  193.2 2.2 fusion.68
  196.2 17.9 %reduce-scatter.13.cloned.1.call-done = bf16[128,256]{1,0:T(8,128)(2,1)} async-done(((bf16[128,1024]{1,0:T(8,128)(2,1)}), bf16[128,256]{1,0:T(8,128)(2,1)}) %reduce-scatter.13.cloned.1.call-update) | async-done | bytes 65552 | tf_op jit(solution)/shard_map/reduce_scatter | solution.py:58
  214.0 14.2 %all_gather.30 = bf16[128,1024]{1,0:T(8,128)(2,1)S(1)} all-gather(bf16[128,256]{1,0:T(8,128)(2,1)} %reduce-scatter.13.cloned.1.call-done), channel_id=1, replica_groups=mesh['section'=4,'dp'=2,'tensor'=4] {'tensor'}, dimensions={1}, use_global_device_ids=true | all-gather | bytes 327680 | tf_op jit(solution)/shard_map/all_gather | solution.py:61
  228.2 4.0 %bitcast_dynamic-update-slice_fusion = (bf16[2,128,2048]{2,1,0:T(8,128)(2,1)S(1)}, bf16[128,2048]{1,0:T(8,128)(2,1)S(1)}) fusion(bf16[2,128,2048]{2,1,0:T(8,128)(2,1)S(1)} %get-tuple-element.21, s32[]{:T(128)S(6)} %min.19, bf16[1,128,2048]{2,1,0:T(8,128)(2,1)} %constant_dynamic-slice_fusion, pred[]{:T(512)S(6)} %and.20, ...), kind=kOutput, calls=%fused_computation.74 | convolution fusion | flops 537657344 | bytes 7077893 | tf_op jit(solution)/shard_map/tr,dr->td/dot_general | solution.py:77
  232.3 1.4 collective-permute-start.3
  235.3 8.4 %collective-permute-done.3 = bf16[128,2048]{1,0:T(8,128)(2,1)S(1)} collective-permute-done((bf16[128,2048]{1,0:T(8,128)(2,1)S(1)}, bf16[128,2048]{1,0:T(8,128)(2,1)S(1)}, u32[]{:S(2)}, u32[]{:S(2)}) %collective-permute-start.3) | collective-permute-done | bytes 524320 | tf_op jit(solution)/shard_map/ppermute | solution.py:10
  245.1 4.4 %fusion.71 = bf16[128,1024]{1,0:T(8,128)(2,1)} fusion(bf16[1,1024,2048]{2,1,0:T(8,128)(2,1)} %all-gather.6.cloned.1.call-done, bf16[128,2048]{1,0:T(8,128)(2,1)S(1)} %collective-permute-done.3, bf16[2,128,2048]{2,1,0:T(8,128)(2,1)S(1)} %copy-done.3, s32[]{:T(128)S(6)} %min.20, pred[]{:T(512)S(6)} %eq.14), kind=kOutput, calls=%fused_computation.37 | convolution fusion | flops 537264128 | bytes 5505029 | tf_op jit(solution)/shard_map/td,rd->tr/dot_general | solution.py:55
  251.2 1.4 bitcast_convert_fusion
  252.5 22.0 %reduce-scatter.15.cloned.1.call-done = bf16[128,256]{1,0:T(8,128)(2,1)} async-done(((bf16[128,1024]{1,0:T(8,128)(2,1)}), bf16[128,256]{1,0:T(8,128)(2,1)}) %reduce-scatter.15.cloned.1.call-update) | async-done | bytes 65552 | tf_op jit(solution)/shard_map/reduce_scatter | solution.py:58
  274.5 14.2 %all_gather.31 = bf16[128,1024]{1,0:T(8,128)(2,1)S(1)} all-gather(bf16[128,256]{1,0:T(8,128)(2,1)} %reduce-scatter.15.cloned.1.call-done), channel_id=1, replica_groups=mesh['section'=4,'dp'=2,'tensor'=4] {'tensor'}, dimensions={1}, use_global_device_ids=true | all-gather | bytes 327680 | tf_op jit(solution)/shard_map/all_gather | solution.py:61
  288.7 4.7 %fusion.56 = bf16[1,2,128,2048]{3,2,1,0:T(8,128)(2,1)} fusion(bf16[1,2,128,2048]{3,2,1,0:T(8,128)(2,1)} %copy.135, s32[]{:T(128)S(6)} %min.20, bf16[128,1024]{1,0:T(8,128)(2,1)S(1)} %all_gather.31, bf16[1,2048,1024]{2,1,0:T(8,128)(2,1)} %all-gather.8.cloned.1.call-done, f32[16,8,16,128]{3,2,1,0:T(8,128)S(1)} %bitcast.276, ...), kind=kOutput, calls=%fused_computation.32 | convolution fusion | flops 537657344 | bytes 6553605 | tf_op jit(solution)/shard_map/tr,dr->td/dot_general | solution.py:77
  (105 shorter events, 26.9 us)
Async XLA Ops:
  7.2 18.8 %all-gather.6.cloned.1.call-start = ((), (), s32[]{:S(2)}) async-start(), calls=%async_computation.12 | async-start | bytes 6291456 | tf_op jit(solution)/shard_map/all_gather | solution.py:24
  7.9 23.4 %copy-start.3 = (bf16[2,128,2048]{2,1,0:T(8,128)(2,1)S(1)}, bf16[2,128,2048]{2,1,0:T(8,128)(2,1)}, u32[]{:S(2)}) copy-start(bf16[2,128,2048]{2,1,0:T(8,128)(2,1)} %param.7) | copy-start | bytes 3145732
  7.9 44.0 %reduce-scatter.7.cloned.1.call-start = ((), (), s32[]{:S(2)}) async-start(), calls=%async_computation.6 | async-start | bytes 327680 | tf_op jit(solution)/shard_map/reduce_scatter | solution.py:58
  8.0 24.1 %copy-start.13 = (s32[1,8]{1,0:T(1,128)S(1)}, s32[1,8]{1,0:T(1,128)}, u32[]{:S(2)}) copy-start(s32[1,8]{1,0:T(1,128)} %param.12) | copy-start | bytes 100
  8.0 24.8 %copy-start.14 = (s32[1,8]{1,0:T(1,128)S(1)}, s32[1,8]{1,0:T(1,128)}, u32[]{:S(2)}) copy-start(s32[1,8]{1,0:T(1,128)} %param.13) | copy-start | bytes 100
  8.0 25.6 %copy-start.4 = (bf16[1,2,128,2048]{3,2,1,0:T(8,128)(2,1)S(1)}, bf16[1,2,128,2048]{3,2,1,0:T(8,128)(2,1)}, u32[]{:S(2)}) copy-start(bf16[1,2,128,2048]{3,2,1,0:T(8,128)(2,1)} %param.8) | copy-start | bytes 3145732
  30.5 35.3 %all-gather.8.cloned.1.call-start = ((), (), s32[]{:S(2)}) async-start(), calls=%async_computation.13 | async-start | bytes 6291456 | tf_op jit(solution)/shard_map/all_gather | solution.py:25
  31.3 79.2 %reduce-scatter.9.cloned.1.call-start = ((), (), s32[]{:S(2)}) async-start(), calls=%async_computation.7 | async-start | bytes 327680 | tf_op jit(solution)/shard_map/reduce_scatter | solution.py:58
  31.3 4.8 %copy-start.12 = (bf16[1,1,128,128]{3,2,1,0:T(8,128)(2,1)S(1)}, bf16[1,1,128,128]{3,2,1,0:T(8,128)(2,1)}, u32[]{:S(2)}) copy-start(bf16[1,1,128,128]{3,2,1,0:T(8,128)(2,1)} %param.11) | copy-start | bytes 98308
  70.7 15.7 %collective-permute-start = (bf16[128,2048]{1,0:T(8,128)(2,1)}, bf16[128,2048]{1,0:T(8,128)(2,1)S(1)}, u32[]{:S(2)}, u32[]{:S(2)}) collective-permute-start(bf16[128,2048]{1,0:T(8,128)(2,1)} %get-tuple-element.18), channel_id=1, source_target_pairs={{8,0},{16,8},{24,16},{9,1},{17,9},{25,17},{10,2},{18,10},{26,18},{... | collective-permute-start | bytes 1572872 | tf_op jit(solution)/shard_map/ppermute | solution.py:10
  77.1 9.7 %copy-start = (bf16[1,1024,2048]{2,1,0:T(8,128)(2,1)S(1)}, bf16[1,1024,2048]{2,1,0:T(8,128)(2,1)}, u32[]{:S(2)}) copy-start(bf16[1,1024,2048]{2,1,0:T(8,128)(2,1)} %all-gather.6.cloned.1.call-done) | copy-start | bytes 12582916
  89.1 73.1 %reduce-scatter.11.cloned.1.call-start = ((), (), s32[]{:S(2)}) async-start(), calls=%async_computation.8 | async-start | bytes 327680 | tf_op jit(solution)/shard_map/reduce_scatter | solution.py:58
  110.4 20.3 %copy-start.5 = (bf16[16,8,16,128]{3,2,1,0:T(8,128)(2,1)S(1)}, bf16[16,8,16,128]{3,2,1,0:T(8,128)(2,1)}, u32[]{:S(2)}) copy-start(bf16[16,8,16,128]{3,2,1,0:T(8,128)(2,1)} %copy.73) | copy-start | bytes 1572868
  129.4 11.6 %collective-permute-start.1 = (bf16[128,2048]{1,0:T(8,128)(2,1)}, bf16[128,2048]{1,0:T(8,128)(2,1)S(1)}, u32[]{:S(2)}, u32[]{:S(2)}) collective-permute-start(bf16[128,2048]{1,0:T(8,128)(2,1)} %get-tuple-element.20), channel_id=1, source_target_pairs={{8,0},{16,8},{24,16},{9,1},{17,9},{25,17},{10,2},{18,10},{26,18},{... | collective-permute-start | bytes 1572872 | tf_op jit(solution)/shard_map/ppermute | solution.py:10
  132.8 8.7 %copy-start.1 = (bf16[1,1024,2048]{2,1,0:T(8,128)(2,1)S(1)}, bf16[1,1024,2048]{2,1,0:T(8,128)(2,1)}, u32[]{:S(2)}) copy-start(bf16[1,1024,2048]{2,1,0:T(8,128)(2,1)} %all-gather.6.cloned.1.call-done) | copy-start | bytes 12582916
  143.7 70.3 %reduce-scatter.13.cloned.1.call-start = ((), (), s32[]{:S(2)}) async-start(), calls=%async_computation.9 | async-start | bytes 327680 | tf_op jit(solution)/shard_map/reduce_scatter | solution.py:58
  144.4 38.3 %copy-start.9 = (bf16[128,2,128]{2,1,0:T(2,128)(2,1)S(1)}, bf16[128,2,128]{2,1,0:T(2,128)(2,1)}, u32[]{:S(2)}) copy-start(bf16[128,2,128]{2,1,0:T(2,128)(2,1)} %fusion.81) | copy-start | bytes 196612
  181.4 11.4 %collective-permute-start.2 = (bf16[128,2048]{1,0:T(8,128)(2,1)}, bf16[128,2048]{1,0:T(8,128)(2,1)S(1)}, u32[]{:S(2)}, u32[]{:S(2)}) collective-permute-start(bf16[128,2048]{1,0:T(8,128)(2,1)} %get-tuple-element.22), channel_id=1, source_target_pairs={{8,0},{16,8},{24,16},{9,1},{17,9},{25,17},{10,2},{18,10},{26,18},{... | collective-permute-start | bytes 1572872 | tf_op jit(solution)/shard_map/ppermute | solution.py:10
  184.7 8.5 %copy-start.2 = (bf16[1,1024,2048]{2,1,0:T(8,128)(2,1)S(1)}, bf16[1,1024,2048]{2,1,0:T(8,128)(2,1)}, u32[]{:S(2)}) copy-start(bf16[1,1024,2048]{2,1,0:T(8,128)(2,1)} %all-gather.6.cloned.1.call-done) | copy-start | bytes 12582916
  195.5 55.6 %reduce-scatter.17.cloned.1.call-start = ((), (), s32[]{:S(2)}) async-start(), calls=%async_computation.11 | async-start | bytes 98304 | tf_op jit(solution)/shard_map/reduce_scatter | solution.py:101
  195.8 37.9 %copy-start.6 = (f32[2,128,128]{2,1,0:T(8,128)S(1)}, f32[2,128,128]{2,1,0:T(8,128)}, u32[]{:S(2)}) copy-start(f32[2,128,128]{2,1,0:T(8,128)} %fusion.116) | copy-start | bytes 393220
  214.0 19.7 %copy-start.8 = (bf16[128,2,128]{2,1,0:T(2,128)(2,1)S(1)}, bf16[128,2,128]{2,1,0:T(2,128)(2,1)}, u32[]{:S(2)}) copy-start(bf16[128,2,128]{2,1,0:T(2,128)(2,1)} %fusion.83) | copy-start | bytes 196612
  214.0 19.9 %copy-start.10 = (bf16[128,2,128]{2,1,0:T(2,128)(2,1)S(1)}, bf16[128,2,128]{2,1,0:T(2,128)(2,1)}, u32[]{:S(2)}) copy-start(bf16[128,2,128]{2,1,0:T(2,128)(2,1)} %fusion.85) | copy-start | bytes 196612
  214.0 20.1 %copy-start.11 = (bf16[128,2,128]{2,1,0:T(2,128)(2,1)S(1)}, bf16[128,2,128]{2,1,0:T(2,128)(2,1)}, u32[]{:S(2)}) copy-start(bf16[128,2,128]{2,1,0:T(2,128)(2,1)} %fusion.87) | copy-start | bytes 196612
  232.2 12.0 %copy-start.7 = (bf16[128,2,128]{2,1,0:T(2,128)(2,1)S(1)}, bf16[128,2,128]{2,1,0:T(2,128)(2,1)}, u32[]{:S(2)}) copy-start(bf16[128,2,128]{2,1,0:T(2,128)(2,1)} %fusion.89) | copy-start | bytes 196612
  232.3 11.5 %collective-permute-start.3 = (bf16[128,2048]{1,0:T(8,128)(2,1)S(1)}, bf16[128,2048]{1,0:T(8,128)(2,1)S(1)}, u32[]{:S(2)}, u32[]{:S(2)}) collective-permute-start(bf16[128,2048]{1,0:T(8,128)(2,1)S(1)} %get-tuple-element.24), channel_id=1, source_target_pairs={{8,0},{16,8},{24,16},{9,1},{17,9},{25,17},{10,2},{18,10},{26,18},{... | collective-permute-start | bytes 1572872 | tf_op jit(solution)/shard_map/ppermute | solution.py:10
  245.1 29.4 %reduce-scatter.15.cloned.1.call-start = ((), (), s32[]{:S(2)}) async-start(), calls=%async_computation.10 | async-start | bytes 327680 | tf_op jit(solution)/shard_map/reduce_scatter | solution.py:58
Sparse Core Ops, SparseCore 0:
  9.5 16.3 all-gather.5
  30.7 21.1 reduce-scatter.6
  53.4 11.8 all-gather.7
  89.2 21.1 reduce-scatter.8
  143.8 18.3 reduce-scatter.10
  195.6 18.3 reduce-scatter.12
  245.2 5.9 reduce-scatter.16
  253.4 21.0 reduce-scatter.14
where the time goes:
time: 301 us; the launch traced here: 300 us
  waiting for transfers between devices  140 us (47%)
  blocking collectives  72.7 us (24%)
  matrix products  51 us (17%)
  between operations  14.6 us (5%)
  local copies, waits for them, and re-layouts  12.8 us (4%)
  starting transfers between devices  5.59 us (2%)
  other arithmetic  3.35 us (1%)
    reduce_scatter x5, waiting for transfers between devices, on_device(): lax.psum_scatter(partial_value.astype(jnp.bfloat16), 'tensor', scatter_di...  91.2 us
    all_gather x5, blocking collectives, on_device(): rank_act = lax.all_gather(share, 'tensor', axis=1, tiled=True)  70.8 us
    ppermute x4, waiting for transfers between devices, shifted(): lax.ppermute(value, axis, [(source, source + steps) for source in range(i...  28.5 us
    dot_general x5, matrix products, on_device(): jnp.einsum('tr,dr->td', rank_act, right_full, preferred_element_type=jnp....  23.1 us
    all_gather x1, waiting for transfers between devices, on_device(): lax.all_gather(factor_a[0], 'dp', axis=0, tiled=True)  17.9 us
    dot_general x5, matrix products, on_device(): jnp.einsum('td,rd->tr', cot_now, left_full, preferred_element_type=jnp.fl...  15.7 us
    unnamed x43, local copies, waits for them, and re-layouts  9.95 us
  transfers between devices with their start and end apart: 12, of which 11 were waited for; matrix products, arithmetic and copies ran while one was open for 10% of the time, Pallas kernels for 0%

commit v1 on v0

--- a/solution.py
+++ b/solution.py
@@ -1,7 +1,25 @@
+import functools
 import jax
 import jax.numpy as jnp
 from jax import lax
 from jax.sharding import PartitionSpec as P
+
+
+def view_the_clusters(arr, axis_name):
+    n_chips = lax.axis_size(axis_name)
+    nodes = []
+    for j in range(n_chips):
+        nodes.append((j, (j + 1) % n_chips))
+    row_out = [None] * n_chips
+    row_out[n_chips - 1] = arr
+    for i in range(n_chips - 2, -1, -1):
+        row_out[i] = lax.ppermute(row_out[i + 1], axis_name=axis_name, perm=nodes)
+    big = jnp.concatenate(row_out, 1)
+    tile_out = (lax.axis_index(axis_name) + 1) * arr.shape[1]
+    return jnp.roll(big, tile_out, axis=1)
+
+
+_touch_hubs = functools.partial(view_the_clusters, axis_name="tensor")
 
 
 def shifted(value, axis, steps):
@@ -58,7 +76,7 @@
         share = lax.psum_scatter(
             partial_value.astype(jnp.bfloat16), "tensor", scatter_dimension=1, tiled=True
         )
-        rank_act = lax.all_gather(share, "tensor", axis=1, tiled=True)
+        rank_act = _touch_hubs(share)
         picked_cot = jnp.einsum(
             "tlc,nl->tnc",
             cot_now.reshape(tokens_here, local_blocks, block_size),

time: 301 us -> 315 us (1.047)
  waiting for transfers between devices: 140 us -> 220 us
  blocking collectives: 72.7 us -> 1.85 us
  matrix products: 51 us -> 57.5 us
  local copies, waits for them, and re-layouts: 12.8 us -> 8.54 us
  other arithmetic: 3.35 us -> 6.5 us
    ppermute x0 -> x15, waiting for transfers between devices: none -> 89.2 us  [view_the_clusters(): row_out[i] = lax.ppermute(row_out[i + 1], axis_name=axis_name, perm=nodes)]
    all_gather x5 -> x0, blocking collectives: 70.8 us -> none  [on_device(): rank_act = lax.all_gather(share, 'tensor', axis=1, tiled=True)]
    reduce_scatter x5, waiting for transfers between devices: 91.2 us -> 83.9 us  [on_device(): lax.psum_scatter(partial_value.astype(jnp.bfloat16), 'tensor', scatter_di...]
    dot_general x5, matrix products: 15.7 us -> 20.5 us  [on_device(): jnp.einsum('td,rd->tr', cot_now, left_full, preferred_element_type=jnp.fl...]
    unnamed x43, local copies, waits for them, and re-layouts: 9.95 us -> 6.54 us
  transfers between devices with their start and end apart: 12 -> 27, of which waited for: 11 -> 25; matrix products, arithmetic and copies ran while one was open for 10% -> 9% of each run, Pallas kernels for 0% -> 0%
where the time goes in v1:
time: 315 us
  waiting for transfers between devices  220 us (70%)
  matrix products  57.5 us (18%)
  between operations  14.6 us (5%)
  local copies, waits for them, and re-layouts  8.54 us (3%)
  other arithmetic  6.5 us (2%)
  starting transfers between devices  5.76 us (2%)
    ppermute x15, waiting for transfers between devices, view_the_clusters(): row_out[i] = lax.ppermute(row_out[i + 1], axis_name=axis_name, perm=nodes)  89.2 us
    reduce_scatter x5, waiting for transfers between devices, on_device(): lax.psum_scatter(partial_value.astype(jnp.bfloat16), 'tensor', scatter_di...  83.9 us
    ppermute x4, waiting for transfers between devices, shifted(): lax.ppermute(value, axis, [(source, source + steps) for source in range(i...  27.6 us
    dot_general x5, matrix products, on_device(): jnp.einsum('tr,dr->td', rank_act, right_full, preferred_element_type=jnp....  24 us
    dot_general x5, matrix products, on_device(): jnp.einsum('td,rd->tr', cot_now, left_full, preferred_element_type=jnp.fl...  20.5 us
    all_gather x1, waiting for transfers between devices, on_device(): lax.all_gather(factor_a[0], 'dp', axis=0, tiled=True)  17.9 us
    unnamed x43, local copies, waits for them, and re-layouts  6.54 us
  transfers between devices with their start and end apart: 27, of which 25 were waited for; matrix products, arithmetic and copies ran while one was open for 9% of the time, Pallas kernels for 0%

profile of v1, /device:TPU:0, one launch (start us, length us, event | category | flops | bytes accessed | tf_op | source)
XLA Modules:
  0.0 314.9 jit_solution(6753509634754021329)
XLA Ops:
  8.0 17.9 %all-gather.6.cloned.1.call-done = bf16[1,1024,2048]{2,1,0:T(8,128)(2,1)} async-done(((bf16[1,512,2048]{2,1,0:T(8,128)(2,1)}), bf16[1,1024,2048]{2,1,0:T(8,128)(2,1)}) %all-gather.6.cloned.1.call-update) | async-done | bytes 4194320 | tf_op jit(solution)/shard_map/all_gather | solution.py:42
  25.9 4.6 %fusion.59 = bf16[128,1024]{1,0:T(8,128)(2,1)} fusion(bf16[1,1024,2048]{2,1,0:T(8,128)(2,1)} %all-gather.6.cloned.1.call-done, bf16[2,128,2048]{2,1,0:T(8,128)(2,1)} %param.9, s32[]{:T(128)S(6)} %min.16, pred[]{:T(512)S(6)} %eq.15), kind=kOutput, calls=%fused_computation.33 | convolution fusion | flops 537264128 | bytes 4980741 | tf_op jit(solution)/shard_map/td,rd->tr/dot_general | solution.py:73
  36.1 15.8 %reduce-scatter.7.cloned.1.call-done = bf16[128,256]{1,0:T(8,128)(2,1)} async-done(((bf16[128,1024]{1,0:T(8,128)(2,1)}), bf16[128,256]{1,0:T(8,128)(2,1)}) %reduce-scatter.7.cloned.1.call-update) | async-done | bytes 65552 | tf_op jit(solution)/shard_map/reduce_scatter | solution.py:76
  51.9 6.2 %collective-permute-done = bf16[128,256]{1,0:T(8,128)(2,1)S(1)} collective-permute-done((bf16[128,256]{1,0:T(8,128)(2,1)}, bf16[128,256]{1,0:T(8,128)(2,1)S(1)}, u32[]{:S(2)}, u32[]{:S(2)}) %collective-permute-start) | collective-permute-done | bytes 65568 | tf_op jit(solution)/shard_map/ppermute | solution.py:16
  58.2 6.5 %collective-permute-done.1 = bf16[128,256]{1,0:T(8,128)(2,1)S(1)} collective-permute-done((bf16[128,256]{1,0:T(8,128)(2,1)S(1)}, bf16[128,256]{1,0:T(8,128)(2,1)S(1)}, u32[]{:S(2)}, u32[]{:S(2)}) %collective-permute-start.1) | collective-permute-done | bytes 65568 | tf_op jit(solution)/shard_map/ppermute | solution.py:16
  66.0 4.7 %collective-permute-done.2 = bf16[128,256]{1,0:T(8,128)(2,1)S(1)} collective-permute-done((bf16[128,256]{1,0:T(8,128)(2,1)S(1)}, bf16[128,256]{1,0:T(8,128)(2,1)S(1)}, u32[]{:S(2)}, u32[]{:S(2)}) %collective-permute-start.2) | collective-permute-done | bytes 65568 | tf_op jit(solution)/shard_map/ppermute | solution.py:16
  70.8 5.2 %bitcast_dynamic-update-slice_fusion.3 = (bf16[2,128,2048]{2,1,0:T(8,128)(2,1)S(1)}, bf16[128,2048]{1,0:T(8,128)(2,1)}) fusion(bf16[2,128,2048]{2,1,0:T(8,128)(2,1)S(1)} %broadcast_in_dim.36, s32[]{:T(128)S(6)} %min.16, pred[]{:T(512)S(6)} %and.22, f32[16,8,16,128]{3,2,1,0:T(8,128)} %bitcast.281, bf16[1,2048,1024]{2,1,0:T(8,128)(2,1)} %all-gather.8.cloned.1.call-done, ...), kind=kOutput, calls=%fused_computation.123 | convolution fusion | flops 539754496 | bytes 6553609 | tf_op jit(solution)/shard_map/tr,dr->td/dot_general | solution.py:95
  79.7 7.7 %collective-permute-done.3 = bf16[128,2048]{1,0:T(8,128)(2,1)} collective-permute-done((bf16[128,2048]{1,0:T(8,128)(2,1)}, bf16[128,2048]{1,0:T(8,128)(2,1)}, u32[]{:S(2)}, u32[]{:S(2)}) %collective-permute-start.3) | collective-permute-done | bytes 524320 | tf_op jit(solution)/shard_map/ppermute | solution.py:28
  87.4 4.6 %fusion.62 = bf16[128,1024]{1,0:T(8,128)(2,1)} fusion(bf16[1,1024,2048]{2,1,0:T(8,128)(2,1)} %all-gather.6.cloned.1.call-done, bf16[128,2048]{1,0:T(8,128)(2,1)} %collective-permute-done.3, bf16[2,128,2048]{2,1,0:T(8,128)(2,1)S(1)} %copy-done.1, s32[]{:T(128)S(6)} %min.17, pred[]{:T(512)S(6)} %eq.15), kind=kOutput, calls=%fused_computation.34 | convolution fusion | flops 537264128 | bytes 5505029 | tf_op jit(solution)/shard_map/td,rd->tr/dot_general | solution.py:73
  94.4 18.5 %reduce-scatter.9.cloned.1.call-done = bf16[128,256]{1,0:T(8,128)(2,1)} async-done(((bf16[128,1024]{1,0:T(8,128)(2,1)}), bf16[128,256]{1,0:T(8,128)(2,1)}) %reduce-scatter.9.cloned.1.call-update) | async-done | bytes 65552 | tf_op jit(solution)/shard_map/reduce_scatter | solution.py:76
  113.1 6.1 %collective-permute-done.4 = bf16[128,256]{1,0:T(8,128)(2,1)S(1)} collective-permute-done((bf16[128,256]{1,0:T(8,128)(2,1)}, bf16[128,256]{1,0:T(8,128)(2,1)S(1)}, u32[]{:S(2)}, u32[]{:S(2)}) %collective-permute-start.4) | collective-permute-done | bytes 65568 | tf_op jit(solution)/shard_map/ppermute | solution.py:16
  119.2 6.5 %collective-permute-done.5 = bf16[128,256]{1,0:T(8,128)(2,1)S(1)} collective-permute-done((bf16[128,256]{1,0:T(8,128)(2,1)S(1)}, bf16[128,256]{1,0:T(8,128)(2,1)S(1)}, u32[]{:S(2)}, u32[]{:S(2)}) %collective-permute-start.5) | collective-permute-done | bytes 65568 | tf_op jit(solution)/shard_map/ppermute | solution.py:16
  126.1 5.7 %collective-permute-done.6 = bf16[128,256]{1,0:T(8,128)(2,1)S(1)} collective-permute-done((bf16[128,256]{1,0:T(8,128)(2,1)S(1)}, bf16[128,256]{1,0:T(8,128)(2,1)S(1)}, u32[]{:S(2)}, u32[]{:S(2)}) %collective-permute-start.6) | collective-permute-done | bytes 65568 | tf_op jit(solution)/shard_map/ppermute | solution.py:16
  131.8 5.0 %bitcast_dynamic-update-slice_fusion.2 = (bf16[2,128,2048]{2,1,0:T(8,128)(2,1)S(1)}, bf16[128,2048]{1,0:T(8,128)(2,1)}) fusion(bf16[2,128,2048]{2,1,0:T(8,128)(2,1)S(1)} %get-tuple-element.18, s32[]{:T(128)S(6)} %min.17, bf16[1,128,2048]{2,1,0:T(8,128)(2,1)} %constant_dynamic-slice_fusion.2, pred[]{:T(512)S(6)} %and.23, ...), kind=kOutput, calls=%fused_computation.120 | convolution fusion | flops 539754496 | bytes 7077897 | tf_op jit(solution)/shard_map/tr,dr->td/dot_general | solution.py:95
  142.9 5.2 %collective-permute-done.7 = bf16[128,2048]{1,0:T(8,128)(2,1)} collective-permute-done((bf16[128,2048]{1,0:T(8,128)(2,1)}, bf16[128,2048]{1,0:T(8,128)(2,1)}, u32[]{:S(2)}, u32[]{:S(2)}) %collective-permute-start.7) | collective-permute-done | bytes 524320 | tf_op jit(solution)/shard_map/ppermute | solution.py:28
  155.2 15.8 %reduce-scatter.11.cloned.1.call-done = bf16[128,256]{1,0:T(8,128)(2,1)} async-done(((bf16[128,1024]{1,0:T(8,128)(2,1)}), bf16[128,256]{1,0:T(8,128)(2,1)}) %reduce-scatter.11.cloned.1.call-update) | async-done | bytes 65552 | tf_op jit(solution)/shard_map/reduce_scatter | solution.py:76
  171.2 6.1 %collective-permute-done.8 = bf16[128,256]{1,0:T(8,128)(2,1)S(1)} collective-permute-done((bf16[128,256]{1,0:T(8,128)(2,1)}, bf16[128,256]{1,0:T(8,128)(2,1)S(1)}, u32[]{:S(2)}, u32[]{:S(2)}) %collective-permute-start.8) | collective-permute-done | bytes 65568 | tf_op jit(solution)/shard_map/ppermute | solution.py:16
  177.3 6.5 %collective-permute-done.9 = bf16[128,256]{1,0:T(8,128)(2,1)S(1)} collective-permute-done((bf16[128,256]{1,0:T(8,128)(2,1)S(1)}, bf16[128,256]{1,0:T(8,128)(2,1)S(1)}, u32[]{:S(2)}, u32[]{:S(2)}) %collective-permute-start.9) | collective-permute-done | bytes 65568 | tf_op jit(solution)/shard_map/ppermute | solution.py:16
  184.2 5.6 %collective-permute-done.10 = bf16[128,256]{1,0:T(8,128)(2,1)S(1)} collective-permute-done((bf16[128,256]{1,0:T(8,128)(2,1)S(1)}, bf16[128,256]{1,0:T(8,128)(2,1)S(1)}, u32[]{:S(2)}, u32[]{:S(2)}) %collective-permute-start.10) | collective-permute-done | bytes 65568 | tf_op jit(solution)/shard_map/ppermute | solution.py:16
  189.8 5.0 %bitcast_dynamic-update-slice_fusion.1 = (bf16[2,128,2048]{2,1,0:T(8,128)(2,1)S(1)}, bf16[128,2048]{1,0:T(8,128)(2,1)}) fusion(bf16[2,128,2048]{2,1,0:T(8,128)(2,1)S(1)} %get-tuple-element.20, s32[]{:T(128)S(6)} %min.18, bf16[1,128,2048]{2,1,0:T(8,128)(2,1)} %constant_dynamic-slice_fusion.1, pred[]{:T(512)S(6)} %and.24, ...), kind=kOutput, calls=%fused_computation.117 | convolution fusion | flops 539754496 | bytes 7077897 | tf_op jit(solution)/shard_map/tr,dr->td/dot_general | solution.py:95
  199.6 6.6 %collective-permute-done.11 = bf16[128,2048]{1,0:T(8,128)(2,1)} collective-permute-done((bf16[128,2048]{1,0:T(8,128)(2,1)}, bf16[128,2048]{1,0:T(8,128)(2,1)}, u32[]{:S(2)}, u32[]{:S(2)}) %collective-permute-start.11) | collective-permute-done | bytes 524320 | tf_op jit(solution)/shard_map/ppermute | solution.py:28
  206.2 4.6 %fusion.68 = bf16[128,1024]{1,0:T(8,128)(2,1)} fusion(bf16[1,1024,2048]{2,1,0:T(8,128)(2,1)} %all-gather.6.cloned.1.call-done, bf16[128,2048]{1,0:T(8,128)(2,1)} %collective-permute-done.11, bf16[2,128,2048]{2,1,0:T(8,128)(2,1)S(1)} %copy-done.1, s32[]{:T(128)S(6)} %min.19, pred[]{:T(512)S(6)} %eq.15), kind=kOutput, calls=%fused_computation.36 | convolution fusion | flops 537264128 | bytes 5505029 | tf_op jit(solution)/shard_map/td,rd->tr/dot_general | solution.py:73
  212.5 16.7 %reduce-scatter.13.cloned.1.call-done = bf16[128,256]{1,0:T(8,128)(2,1)} async-done(((bf16[128,1024]{1,0:T(8,128)(2,1)}), bf16[128,256]{1,0:T(8,128)(2,1)}) %reduce-scatter.13.cloned.1.call-update) | async-done | bytes 65552 | tf_op jit(solution)/shard_map/reduce_scatter | solution.py:76
  229.3 6.1 %collective-permute-done.12 = bf16[128,256]{1,0:T(8,128)(2,1)S(1)} collective-permute-done((bf16[128,256]{1,0:T(8,128)(2,1)}, bf16[128,256]{1,0:T(8,128)(2,1)S(1)}, u32[]{:S(2)}, u32[]{:S(2)}) %collective-permute-start.12) | collective-permute-done | bytes 65568 | tf_op jit(solution)/shard_map/ppermute | solution.py:16
  235.5 6.5 %collective-permute-done.13 = bf16[128,256]{1,0:T(8,128)(2,1)S(1)} collective-permute-done((bf16[128,256]{1,0:T(8,128)(2,1)S(1)}, bf16[128,256]{1,0:T(8,128)(2,1)S(1)}, u32[]{:S(2)}, u32[]{:S(2)}) %collective-permute-start.13) | collective-permute-done | bytes 65568 | tf_op jit(solution)/shard_map/ppermute | solution.py:16
  242.4 5.7 %collective-permute-done.14 = bf16[128,256]{1,0:T(8,128)(2,1)S(1)} collective-permute-done((bf16[128,256]{1,0:T(8,128)(2,1)S(1)}, bf16[128,256]{1,0:T(8,128)(2,1)S(1)}, u32[]{:S(2)}, u32[]{:S(2)}) %collective-permute-start.14) | collective-permute-done | bytes 65568 | tf_op jit(solution)/shard_map/ppermute | solution.py:16
  255.3 8.1 %collective-permute-done.15 = bf16[128,2048]{1,0:T(8,128)(2,1)S(1)} collective-permute-done((bf16[128,2048]{1,0:T(8,128)(2,1)S(1)}, bf16[128,2048]{1,0:T(8,128)(2,1)S(1)}, u32[]{:S(2)}, u32[]{:S(2)}) %collective-permute-start.15) | collective-permute-done | bytes 524320 | tf_op jit(solution)/shard_map/ppermute | solution.py:28
  267.3 17.0 %reduce-scatter.15.cloned.1.call-done = bf16[128,256]{1,0:T(8,128)(2,1)} async-done(((bf16[128,1024]{1,0:T(8,128)(2,1)}), bf16[128,256]{1,0:T(8,128)(2,1)}) %reduce-scatter.15.cloned.1.call-update) | async-done | bytes 65552 | tf_op jit(solution)/shard_map/reduce_scatter | solution.py:76
  284.4 6.3 %collective-permute-done.16 = bf16[128,256]{1,0:T(8,128)(2,1)S(1)} collective-permute-done((bf16[128,256]{1,0:T(8,128)(2,1)}, bf16[128,256]{1,0:T(8,128)(2,1)S(1)}, u32[]{:S(2)}, u32[]{:S(2)}) %collective-permute-start.16) | collective-permute-done | bytes 65568 | tf_op jit(solution)/shard_map/ppermute | solution.py:16
  291.0 6.2 %collective-permute-done.17 = bf16[128,256]{1,0:T(8,128)(2,1)S(1)} collective-permute-done((bf16[128,256]{1,0:T(8,128)(2,1)S(1)}, bf16[128,256]{1,0:T(8,128)(2,1)S(1)}, u32[]{:S(2)}, u32[]{:S(2)}) %collective-permute-start.17) | collective-permute-done | bytes 65568 | tf_op jit(solution)/shard_map/ppermute | solution.py:16
  298.6 4.7 %collective-permute-done.18 = bf16[128,256]{1,0:T(8,128)(2,1)S(1)} collective-permute-done((bf16[128,256]{1,0:T(8,128)(2,1)S(1)}, bf16[128,256]{1,0:T(8,128)(2,1)S(1)}, u32[]{:S(2)}, u32[]{:S(2)}) %collective-permute-start.18) | collective-permute-done | bytes 65568 | tf_op jit(solution)/shard_map/ppermute | solution.py:16
  303.2 4.8 %fusion.56 = bf16[1,2,128,2048]{3,2,1,0:T(8,128)(2,1)} fusion(bf16[1,2,128,2048]{3,2,1,0:T(8,128)(2,1)} %copy.135, s32[]{:T(128)S(6)} %min.20, bf16[1,2048,1024]{2,1,0:T(8,128)(2,1)} %all-gather.8.cloned.1.call-done, f32[16,8,16,128]{3,2,1,0:T(8,128)S(1)} %bitcast.282, bf16[2,128,2048]{2,1,0:T(8,128)(2,1)S(1)} %get-tuple-element.24, pred[]{:T(512)S(6)} %and.26, ...), kind=kOutput, calls=%fused_computation.32 | convolution fusion | flops 539754496 | bytes 6553609 | tf_op jit(solution)/shard_map/tr,dr->td/dot_general | solution.py:95
  (130 shorter events, 47.9 us)
Async XLA Ops:
  7.2 18.8 %all-gather.6.cloned.1.call-start = ((), (), s32[]{:S(2)}) async-start(), calls=%async_computation.12 | async-start | bytes 6291456 | tf_op jit(solution)/shard_map/all_gather | solution.py:42
  7.9 23.4 %copy-start.1 = (bf16[2,128,2048]{2,1,0:T(8,128)(2,1)S(1)}, bf16[2,128,2048]{2,1,0:T(8,128)(2,1)}, u32[]{:S(2)}) copy-start(bf16[2,128,2048]{2,1,0:T(8,128)(2,1)} %param.9) | copy-start | bytes 3145732
  7.9 43.9 %reduce-scatter.7.cloned.1.call-start = ((), (), s32[]{:S(2)}) async-start(), calls=%async_computation.6 | async-start | bytes 327680 | tf_op jit(solution)/shard_map/reduce_scatter | solution.py:76
  8.0 24.1 %copy-start.13 = (s32[1,8]{1,0:T(1,128)S(1)}, s32[1,8]{1,0:T(1,128)}, u32[]{:S(2)}) copy-start(s32[1,8]{1,0:T(1,128)} %param.14) | copy-start | bytes 100
  8.0 24.8 %copy-start.14 = (s32[1,8]{1,0:T(1,128)S(1)}, s32[1,8]{1,0:T(1,128)}, u32[]{:S(2)}) copy-start(s32[1,8]{1,0:T(1,128)} %param.15) | copy-start | bytes 100
  8.0 25.8 %copy-start.12 = (bf16[1,1,128,128]{3,2,1,0:T(8,128)(2,1)S(1)}, bf16[1,1,128,128]{3,2,1,0:T(8,128)(2,1)}, u32[]{:S(2)}) copy-start(bf16[1,1,128,128]{3,2,1,0:T(8,128)(2,1)} %param.13) | copy-start | bytes 98308
  30.5 35.5 %all-gather.8.cloned.1.call-start = ((), (), s32[]{:S(2)}) async-start(), calls=%async_computation.13 | async-start | bytes 6291456 | tf_op jit(solution)/shard_map/all_gather | solution.py:43
  31.3 81.6 %reduce-scatter.9.cloned.1.call-start = ((), (), s32[]{:S(2)}) async-start(), calls=%async_computation.7 | async-start | bytes 327680 | tf_op jit(solution)/shard_map/reduce_scatter | solution.py:76
  51.9 6.3 %collective-permute-start = (bf16[128,256]{1,0:T(8,128)(2,1)}, bf16[128,256]{1,0:T(8,128)(2,1)S(1)}, u32[]{:S(2)}, u32[]{:S(2)}) collective-permute-start(bf16[128,256]{1,0:T(8,128)(2,1)} %reduce-scatter.7.cloned.1.call-done), channel_id=1, source_target_pairs={{0,1},{1,2},{2,3},{3,0},{4,5},{5,6},{6,7},{7,4},{8,9},{9,10},{10,1... | collective-permute-start | bytes 196616 | tf_op jit(solution)/shard_map/ppermute | solution.py:16
  58.1 6.5 %collective-permute-start.1 = (bf16[128,256]{1,0:T(8,128)(2,1)S(1)}, bf16[128,256]{1,0:T(8,128)(2,1)S(1)}, u32[]{:S(2)}, u32[]{:S(2)}) collective-permute-start(bf16[128,256]{1,0:T(8,128)(2,1)S(1)} %collective-permute-done), channel_id=1, source_target_pairs={{0,1},{1,2},{2,3},{3,0},{4,5},{5,6},{6,7},{7,4},{8,9},{9,10},{10,1... | collective-permute-start | bytes 196616 | tf_op jit(solution)/shard_map/ppermute | solution.py:16
  64.6 6.1 %collective-permute-start.2 = (bf16[128,256]{1,0:T(8,128)(2,1)S(1)}, bf16[128,256]{1,0:T(8,128)(2,1)S(1)}, u32[]{:S(2)}, u32[]{:S(2)}) collective-permute-start(bf16[128,256]{1,0:T(8,128)(2,1)S(1)} %collective-permute-done.1), channel_id=1, source_target_pairs={{0,1},{1,2},{2,3},{3,0},{4,5},{5,6},{6,7},{7,4},{8,9},{9,10},{10,1... | collective-permute-start | bytes 196616 | tf_op jit(solution)/shard_map/ppermute | solution.py:16
  76.0 11.4 %collective-permute-start.3 = (bf16[128,2048]{1,0:T(8,128)(2,1)}, bf16[128,2048]{1,0:T(8,128)(2,1)}, u32[]{:S(2)}, u32[]{:S(2)}) collective-permute-start(bf16[128,2048]{1,0:T(8,128)(2,1)} %get-tuple-element.19), channel_id=1, source_target_pairs={{8,0},{16,8},{24,16},{9,1},{17,9},{25,17},{10,2},{18,10},{26,18},{... | collective-permute-start | bytes 1572872 | tf_op jit(solution)/shard_map/ppermute | solution.py:28
  92.0 79.0 %reduce-scatter.11.cloned.1.call-start = ((), (), s32[]{:S(2)}) async-start(), calls=%async_computation.8 | async-start | bytes 327680 | tf_op jit(solution)/shard_map/reduce_scatter | solution.py:76
  112.9 6.3 %collective-permute-start.4 = (bf16[128,256]{1,0:T(8,128)(2,1)}, bf16[128,256]{1,0:T(8,128)(2,1)S(1)}, u32[]{:S(2)}, u32[]{:S(2)}) collective-permute-start(bf16[128,256]{1,0:T(8,128)(2,1)} %reduce-scatter.9.cloned.1.call-done), channel_id=1, source_target_pairs={{0,1},{1,2},{2,3},{3,0},{4,5},{5,6},{6,7},{7,4},{8,9},{9,10},{10,1... | collective-permute-start | bytes 196616 | tf_op jit(solution)/shard_map/ppermute | solution.py:16
  119.2 6.5 %collective-permute-start.5 = (bf16[128,256]{1,0:T(8,128)(2,1)S(1)}, bf16[128,256]{1,0:T(8,128)(2,1)S(1)}, u32[]{:S(2)}, u32[]{:S(2)}) collective-permute-start(bf16[128,256]{1,0:T(8,128)(2,1)S(1)} %collective-permute-done.4), channel_id=1, source_target_pairs={{0,1},{1,2},{2,3},{3,0},{4,5},{5,6},{6,7},{7,4},{8,9},{9,10},{10,1... | collective-permute-start | bytes 196616 | tf_op jit(solution)/shard_map/ppermute | solution.py:16
  125.7 6.1 %collective-permute-start.6 = (bf16[128,256]{1,0:T(8,128)(2,1)S(1)}, bf16[128,256]{1,0:T(8,128)(2,1)S(1)}, u32[]{:S(2)}, u32[]{:S(2)}) collective-permute-start(bf16[128,256]{1,0:T(8,128)(2,1)S(1)} %collective-permute-done.5), channel_id=1, source_target_pairs={{0,1},{1,2},{2,3},{3,0},{4,5},{5,6},{6,7},{7,4},{8,9},{9,10},{10,1... | collective-permute-start | bytes 196616 | tf_op jit(solution)/shard_map/ppermute | solution.py:16
  126.1 12.0 %copy-start.7 = (bf16[16,8,16,128]{3,2,1,0:T(8,128)(2,1)S(1)}, bf16[16,8,16,128]{3,2,1,0:T(8,128)(2,1)}, u32[]{:S(2)}) copy-start(bf16[16,8,16,128]{3,2,1,0:T(8,128)(2,1)} %copy.71) | copy-start | bytes 1572868
  136.8 11.4 %collective-permute-start.7 = (bf16[128,2048]{1,0:T(8,128)(2,1)}, bf16[128,2048]{1,0:T(8,128)(2,1)}, u32[]{:S(2)}, u32[]{:S(2)}) collective-permute-start(bf16[128,2048]{1,0:T(8,128)(2,1)} %get-tuple-element.21), channel_id=1, source_target_pairs={{8,0},{16,8},{24,16},{9,1},{17,9},{25,17},{10,2},{18,10},{26,18},{... | collective-permute-start | bytes 1572872 | tf_op jit(solution)/shard_map/ppermute | solution.py:28
  152.8 76.4 %reduce-scatter.13.cloned.1.call-start = ((), (), s32[]{:S(2)}) async-start(), calls=%async_computation.9 | async-start | bytes 327680 | tf_op jit(solution)/shard_map/reduce_scatter | solution.py:76
  171.0 6.3 %collective-permute-start.8 = (bf16[128,256]{1,0:T(8,128)(2,1)}, bf16[128,256]{1,0:T(8,128)(2,1)S(1)}, u32[]{:S(2)}, u32[]{:S(2)}) collective-permute-start(bf16[128,256]{1,0:T(8,128)(2,1)} %reduce-scatter.11.cloned.1.call-done), channel_id=1, source_target_pairs={{0,1},{1,2},{2,3},{3,0},{4,5},{5,6},{6,7},{7,4},{8,9},{9,10},{10,1... | collective-permute-start | bytes 196616 | tf_op jit(solution)/shard_map/ppermute | solution.py:16
  177.3 6.5 %collective-permute-start.9 = (bf16[128,256]{1,0:T(8,128)(2,1)S(1)}, bf16[128,256]{1,0:T(8,128)(2,1)S(1)}, u32[]{:S(2)}, u32[]{:S(2)}) collective-permute-start(bf16[128,256]{1,0:T(8,128)(2,1)S(1)} %collective-permute-done.8), channel_id=1, source_target_pairs={{0,1},{1,2},{2,3},{3,0},{4,5},{5,6},{6,7},{7,4},{8,9},{9,10},{10,1... | collective-permute-start | bytes 196616 | tf_op jit(solution)/shard_map/ppermute | solution.py:16
  183.8 6.1 %collective-permute-start.10 = (bf16[128,256]{1,0:T(8,128)(2,1)S(1)}, bf16[128,256]{1,0:T(8,128)(2,1)S(1)}, u32[]{:S(2)}, u32[]{:S(2)}) collective-permute-start(bf16[128,256]{1,0:T(8,128)(2,1)S(1)} %collective-permute-done.9), channel_id=1, source_target_pairs={{0,1},{1,2},{2,3},{3,0},{4,5},{5,6},{6,7},{7,4},{8,9},{9,10},{10,1... | collective-permute-start | bytes 196616 | tf_op jit(solution)/shard_map/ppermute | solution.py:16
  194.9 11.4 %collective-permute-start.11 = (bf16[128,2048]{1,0:T(8,128)(2,1)}, bf16[128,2048]{1,0:T(8,128)(2,1)}, u32[]{:S(2)}, u32[]{:S(2)}) collective-permute-start(bf16[128,2048]{1,0:T(8,128)(2,1)} %get-tuple-element.23), channel_id=1, source_target_pairs={{8,0},{16,8},{24,16},{9,1},{17,9},{25,17},{10,2},{18,10},{26,18},{... | collective-permute-start | bytes 1572872 | tf_op jit(solution)/shard_map/ppermute | solution.py:28
  210.8 73.5 %reduce-scatter.15.cloned.1.call-start = ((), (), s32[]{:S(2)}) async-start(), calls=%async_computation.10 | async-start | bytes 327680 | tf_op jit(solution)/shard_map/reduce_scatter | solution.py:76
  229.2 6.3 %collective-permute-start.12 = (bf16[128,256]{1,0:T(8,128)(2,1)}, bf16[128,256]{1,0:T(8,128)(2,1)S(1)}, u32[]{:S(2)}, u32[]{:S(2)}) collective-permute-start(bf16[128,256]{1,0:T(8,128)(2,1)} %reduce-scatter.13.cloned.1.call-done), channel_id=1, source_target_pairs={{0,1},{1,2},{2,3},{3,0},{4,5},{5,6},{6,7},{7,4},{8,9},{9,10},{10,1... | collective-permute-start | bytes 196616 | tf_op jit(solution)/shard_map/ppermute | solution.py:16
  235.4 6.5 %collective-permute-start.13 = (bf16[128,256]{1,0:T(8,128)(2,1)S(1)}, bf16[128,256]{1,0:T(8,128)(2,1)S(1)}, u32[]{:S(2)}, u32[]{:S(2)}) collective-permute-start(bf16[128,256]{1,0:T(8,128)(2,1)S(1)} %collective-permute-done.12), channel_id=1, source_target_pairs={{0,1},{1,2},{2,3},{3,0},{4,5},{5,6},{6,7},{7,4},{8,9},{9,10},{10,1... | collective-permute-start | bytes 196616 | tf_op jit(solution)/shard_map/ppermute | solution.py:16
  242.0 6.1 %collective-permute-start.14 = (bf16[128,256]{1,0:T(8,128)(2,1)S(1)}, bf16[128,256]{1,0:T(8,128)(2,1)S(1)}, u32[]{:S(2)}, u32[]{:S(2)}) collective-permute-start(bf16[128,256]{1,0:T(8,128)(2,1)S(1)} %collective-permute-done.13), channel_id=1, source_target_pairs={{0,1},{1,2},{2,3},{3,0},{4,5},{5,6},{6,7},{7,4},{8,9},{9,10},{10,1... | collective-permute-start | bytes 196616 | tf_op jit(solution)/shard_map/ppermute | solution.py:16
  252.1 11.3 %collective-permute-start.15 = (bf16[128,2048]{1,0:T(8,128)(2,1)S(1)}, bf16[128,2048]{1,0:T(8,128)(2,1)S(1)}, u32[]{:S(2)}, u32[]{:S(2)}) collective-permute-start(bf16[128,2048]{1,0:T(8,128)(2,1)S(1)} %get-tuple-element.25), channel_id=1, source_target_pairs={{8,0},{16,8},{24,16},{9,1},{17,9},{25,17},{10,2},{18,10},{26,18},{... | collective-permute-start | bytes 1572872 | tf_op jit(solution)/shard_map/ppermute | solution.py:28
  265.9 31.3 %reduce-scatter.17.cloned.1.call-start = ((), (), s32[]{:S(2)}) async-start(), calls=%async_computation.11 | async-start | bytes 98304 | tf_op jit(solution)/shard_map/reduce_scatter | solution.py:119
  284.3 6.3 %collective-permute-start.16 = (bf16[128,256]{1,0:T(8,128)(2,1)}, bf16[128,256]{1,0:T(8,128)(2,1)S(1)}, u32[]{:S(2)}, u32[]{:S(2)}) collective-permute-start(bf16[128,256]{1,0:T(8,128)(2,1)} %reduce-scatter.15.cloned.1.call-done), channel_id=1, source_target_pairs={{0,1},{1,2},{2,3},{3,0},{4,5},{5,6},{6,7},{7,4},{8,9},{9,10},{10,1... | collective-permute-start | bytes 196616 | tf_op jit(solution)/shard_map/ppermute | solution.py:16
  290.6 6.6 %collective-permute-start.17 = (bf16[128,256]{1,0:T(8,128)(2,1)S(1)}, bf16[128,256]{1,0:T(8,128)(2,1)S(1)}, u32[]{:S(2)}, u32[]{:S(2)}) collective-permute-start(bf16[128,256]{1,0:T(8,128)(2,1)S(1)} %collective-permute-done.16), channel_id=1, source_target_pairs={{0,1},{1,2},{2,3},{3,0},{4,5},{5,6},{6,7},{7,4},{8,9},{9,10},{10,1... | collective-permute-start | bytes 196616 | tf_op jit(solution)/shard_map/ppermute | solution.py:16
  297.2 6.1 %collective-permute-start.18 = (bf16[128,256]{1,0:T(8,128)(2,1)S(1)}, bf16[128,256]{1,0:T(8,128)(2,1)S(1)}, u32[]{:S(2)}, u32[]{:S(2)}) collective-permute-start(bf16[128,256]{1,0:T(8,128)(2,1)S(1)} %collective-permute-done.17), channel_id=1, source_target_pairs={{0,1},{1,2},{2,3},{3,0},{4,5},{5,6},{6,7},{7,4},{8,9},{9,10},{10,1... | collective-permute-start | bytes 196616 | tf_op jit(solution)/shard_map/ppermute | solution.py:16
  (10 other events, 82.6 us)
Sparse Core Ops, SparseCore 0:
  9.5 16.3 all-gather.5
  30.7 21.1 reduce-scatter.6
  53.4 11.8 all-gather.7
  92.1 20.7 reduce-scatter.8
  152.9 18.0 reduce-scatter.10
  210.9 18.1 reduce-scatter.12
  266.0 18.2 reduce-scatter.14
  287.1 5.7 reduce-scatter.16
